TPU v7x, 512 devices: a whole 4x8x8 slice. The times are simulated.
512 devices in a mesh: segment: 4 (over x), chan: 16 (over y, core), dp: 8 (over z).
Axes of the slice: x: 4, y: 8, z: 8, core: 2. Of those that a mesh axis runs over, the one named last changes fastest.
Arguments:
- grad_top: bfloat16 [8, 1536, 256], P('dp', None, 'chan'), may hold values from -6 to 6
- inputs_one: bfloat16 [4, 8, 1536, 256], P('segment', 'dp', 'chan'), may hold values from -6 to 6
- conv_one: bfloat16 [4, 8, 1536, 256], P('segment', 'dp', 'chan'), may hold values from -130 to 130
- inputs_two: bfloat16 [4, 8, 1536, 256], P('segment', 'dp', 'chan'), may hold values from -6 to 6
- conv_two: bfloat16 [4, 8, 1536, 256], P('segment', 'dp', 'chan'), may hold values from -130 to 130
- proj_weight: bfloat16 [4, 2, 1536, 1536], P('segment', None, 'chan'), may hold values from -0.15625 to 0.15625
- conv_weight: bfloat16 [4, 2, 1536, 432], P('segment', None, 'chan'), may hold values from -0.3125 to 0.3125
- norm_gain: float32 [4, 2, 1536], P('segment', None, 'chan'), may hold values from 0.1 to 1.9
- norm_bias: float32 [4, 2, 1536], P('segment', None, 'chan'), may hold values from -4 to 4
Outputs:
- grad_latent: bfloat16 [4, 8, 1536, 256], P('segment', 'dp', None, 'chan')
- grad_proj: float32 [4, 2, 1536, 1536], P('segment', None, 'chan')
- grad_conv: float32 [4, 2, 1536, 432], P('segment', None, 'chan')
- grad_gain: float32 [4, 2, 1536], P('segment', None, 'chan')
- grad_bias: float32 [4, 2, 1536], P('segment', None, 'chan')
All inputs are finite; a program needn't handle non-finite values.
Results may differ from a plain program's by a relative error of at most 0.009.
Values may be sent and summed in bfloat16 or wider, within the bound.
No kernel may reach another device: no remote copies, remote signals or barrier semaphores. Data moves between devices by JAX's collectives and lax.ppermute only.
A program may use at most 64 MiB of HBM per device.

v0:
```python
import jax
import jax.numpy as jnp
from jax import lax
from jax.sharding import PartitionSpec as P

GS = 48
WW = 64
NORM_EPS = 1e-05


def passed_along(block, axis, distance):
    devices = range(lax.axis_size(axis))
    route = [(i - distance, i) for i in devices if i - distance in devices]
    return lax.ppermute(block, axis, route)


def shifted_cells(values, step_row, step_col, img_width):
    length = values.shape[2]
    margin = img_width + 1
    padded = jnp.pad(values, ((0, 0), (0, 0), (margin, margin)))
    start_at = margin + step_row * img_width + step_col
    part_view = lax.slice_in_dim(padded, start_at, start_at + length, axis=2)
    column = jnp.arange(length, dtype=jnp.int32) % img_width
    inside = (column + step_col >= 0) & (column + step_col < img_width)
    return jnp.where(inside, part_view, jnp.zeros((), values.dtype))


def norm_forward(saved_pre, gain_vec, bias_vec):
    chans, positions = saved_pre.shape
    groups_here = chans // GS
    pre = saved_pre.astype(jnp.float32).reshape(groups_here, GS, positions)
    centre = jnp.mean(pre, axis=(1, 2), keepdims=True)
    varied = jnp.mean(jnp.square(pre - centre), axis=(1, 2), keepdims=True)
    inv_std = lax.rsqrt(varied + NORM_EPS)
    normed = (pre - centre) * inv_std
    gain_grid = gain_vec.reshape(groups_here, GS, 1)
    scaled = normed * gain_grid + bias_vec.reshape(groups_here, GS, 1)
    gate_vals = jax.nn.sigmoid(scaled)
    act_bf = (scaled * gate_vals).astype(jnp.bfloat16).reshape(chans, positions)
    return (normed, scaled, gate_vals, inv_std, gain_grid, act_bf)


def conv_backward(grad_act, norm_state, saved_in, w_conv):
    normed, scaled, gate_vals, inv_std, gain_grid, act_bf = norm_state
    groups_here, _, positions = normed.shape
    chans = groups_here * GS
    grad_act = grad_act.reshape(groups_here, GS, positions)
    grad_norm = grad_act * (gate_vals * (1.0 + scaled * (1.0 - gate_vals)))
    gain_grad = jnp.sum(grad_norm * normed, axis=2).reshape(chans)
    bias_grad = jnp.sum(grad_norm, axis=2).reshape(chans)
    weighted = grad_norm * gain_grid
    first_mean = jnp.mean(weighted, axis=(1, 2), keepdims=True)
    second_mean = jnp.mean(weighted * normed, axis=(1, 2), keepdims=True)
    grad_pre = (inv_std * (weighted - first_mean - normed * second_mean)).astype(jnp.bfloat16)
    saved_grid = saved_in.reshape(groups_here, GS, positions)
    taps_w = w_conv.reshape(groups_here, GS, 9, GS)
    conv_parts = []
    back_sum = jnp.zeros((groups_here, GS, positions), jnp.float32)
    for tap_row in (-1, 0, 1):
        for tap_col in (-1, 0, 1):
            tap_at = 3 * (tap_row + 1) + tap_col + 1
            source = shifted_cells(saved_grid, tap_row, tap_col, WW)
            conv_parts.append(
                jnp.einsum("gop,gjp->goj", grad_pre, source, preferred_element_type=jnp.float32)
            )
            spread_back = jnp.einsum(
                "goj,gop->gjp",
                taps_w[:, :, tap_at, :],
                grad_pre,
                preferred_element_type=jnp.float32,
            )
            back_sum = back_sum + shifted_cells(spread_back, -tap_row, -tap_col, WW)
    conv_grad = jnp.stack(conv_parts, axis=2).reshape(chans, 9 * GS)
    branch = back_sum.reshape(chans, positions).astype(jnp.bfloat16)
    return (branch, conv_grad, gain_grad, bias_grad)


def block_sharded(grad_slab, saved_in, saved_pre, w_proj, w_conv, gain_vec, bias_vec):
    norm_state = norm_forward(saved_pre, gain_vec, bias_vec)
    act_bf = norm_state[5]
    grad_piece = lax.all_gather(grad_slab, "chan", axis=1, tiled=True)
    fresh = jnp.dot(w_proj, grad_piece, preferred_element_type=jnp.float32)
    weight_acc = lax.dot_general(
        act_bf, grad_piece, (((1,), (1,)), ((), ())), preferred_element_type=jnp.float32
    )
    branch, conv_grad, gain_grad, bias_grad = conv_backward(fresh, norm_state, saved_in, w_conv)
    returned = lax.all_to_all(branch, "chan", split_axis=1, concat_axis=0, tiled=True)
    out_slab = (grad_slab.astype(jnp.float32) + returned.astype(jnp.float32)).astype(jnp.bfloat16)
    return (out_slab, (weight_acc, conv_grad, gain_grad, bias_grad))


def take_micro(saved_all, index_at):
    return lax.dynamic_index_in_dim(saved_all[0], index_at, 0, keepdims=False)


def per_device(
    grad_top,
    inputs_one,
    conv_one,
    inputs_two,
    conv_two,
    proj_weight,
    conv_weight,
    norm_gain,
    norm_bias,
):
    segments = lax.axis_size("segment")
    segment_at = lax.axis_index("segment")
    local_mb = grad_top.shape[0]
    chans = conv_one.shape[2]
    width_all = proj_weight.shape[3]
    ticks = local_mb + segments - 1
    initial = (
        jnp.zeros(grad_top.shape[1:], jnp.bfloat16),
        jnp.zeros((1,) + grad_top.shape, jnp.bfloat16),
        jnp.zeros((2, chans, width_all), jnp.float32),
        jnp.zeros((2, chans, 9 * GS), jnp.float32),
        jnp.zeros((2, chans), jnp.float32),
        jnp.zeros((2, chans), jnp.float32),
    )

    def one_tick(tick_at, running):
        received, latent, proj_acc, conv_acc, gain_acc, bias_acc = running
        micro_at = tick_at - (segments - 1 - segment_at)
        is_valid = (micro_at >= 0) & (micro_at < local_mb)
        safe_mb = jnp.clip(micro_at, 0, local_mb - 1)
        top_grad = lax.dynamic_index_in_dim(grad_top, safe_mb, 0, keepdims=False)
        entering = jnp.where(segment_at == segments - 1, top_grad, received)
        mid_grad, grads_two = block_sharded(
            entering,
            take_micro(inputs_two, safe_mb),
            take_micro(conv_two, safe_mb),
            proj_weight[0, 1],
            conv_weight[0, 1],
            norm_gain[0, 1],
            norm_bias[0, 1],
        )
        out_grad, grads_one = block_sharded(
            mid_grad,
            take_micro(inputs_one, safe_mb),
            take_micro(conv_one, safe_mb),
            proj_weight[0, 0],
            conv_weight[0, 0],
            norm_gain[0, 0],
            norm_bias[0, 0],
        )
        weight_mask = is_valid.astype(jnp.float32)
        proj_acc = proj_acc + weight_mask * jnp.stack((grads_one[0], grads_two[0]))
        conv_acc = conv_acc + weight_mask * jnp.stack((grads_one[1], grads_two[1]))
        gain_acc = gain_acc + weight_mask * jnp.stack((grads_one[2], grads_two[2]))
        bias_acc = bias_acc + weight_mask * jnp.stack((grads_one[3], grads_two[3]))
        current = lax.dynamic_index_in_dim(latent[0], safe_mb, 0, keepdims=False)
        kept = jnp.where(is_valid, out_grad, current)
        latent = lax.dynamic_update_index_in_dim(latent, kept[None, None], safe_mb, 1)
        received = passed_along(out_grad, "segment", -1)
        return (received, latent, proj_acc, conv_acc, gain_acc, bias_acc)

    final = lax.fori_loop(0, ticks, one_tick, initial)
    latent = final[1]
    proj_sum, conv_sum, gain_sum, bias_sum = lax.psum(
        (final[2], final[3], final[4], final[5]), "dp"
    )
    return (latent, proj_sum[None], conv_sum[None], gain_sum[None], bias_sum[None])


def solution(mesh):
    return jax.shard_map(
        per_device,
        mesh=mesh,
        in_specs=(
            P("dp", None, "chan"),
            P("segment", "dp", "chan", None),
            P("segment", "dp", "chan", None),
            P("segment", "dp", "chan", None),
            P("segment", "dp", "chan", None),
            P("segment", None, "chan", None),
            P("segment", None, "chan", None),
            P("segment", None, "chan"),
            P("segment", None, "chan"),
        ),
        out_specs=(
            P("segment", "dp", None, "chan"),
            P("segment", None, "chan", None),
            P("segment", None, "chan", None),
            P("segment", None, "chan"),
            P("segment", None, "chan"),
        ),
        check_vma=False,
    )
```

profile of v0, /device:TPU:2, one launch (start us, length us, event | category | flops | bytes accessed | tf_op | source)
XLA Modules:
  0.0 469.4 jit_solution(2428649469921807830)
XLA Ops:
  9.6 357.8 %while.26 = (s32[]{:T(128)}, bf16[1536,16]{0,1:T(8,128)(2,1)S(1)}, bf16[1,1,1536,16]{2,3,1,0:T(8,128)(2,1)}, f32[2,96,1536]{2,1,0:T(8,128)S(1)}, f32[2,96,432]{1...) while((s32[]{:T(128)}, bf16[1536,16]{0,1:T(8,128)(2,1)S(1)}, ...), condition=%wide.region_21.22_spmd.clone, body=%wide.region_0.21_spmd.clone.sunk | while | flops 392720768 | bytes 27672152 | solution.py:158
  14.7 19.7 %all_gather.24 = bf16[1536,256]{0,1:T(8,128)(2,1)S(1)} all-gather(bf16[1536,16]{0,1:T(8,128)(2,1)S(1)} %bitcast_select_fusion.3), channel_id=1, replica_groups=mesh['segment'=4,'chan'=16,'dp'=8] {'chan'}, dimensions={1}, use_global_device_ids=true | all-gather | bytes 835584 | tf_op jit(solution)/shard_map/while/body/eval_jaxpr/all_gather | solution.py:81
  40.7 4.4 all-to-all-start
  53.2 18.4 %all_gather.25 = bf16[1536,256]{0,1:T(8,128)(2,1)S(1)} all-gather(bf16[1536,16]{0,1:T(8,128)(2,1)S(1)} %add_convert_fusion.4), channel_id=1, replica_groups=mesh['segment'=4,'chan'=16,'dp'=8] {'chan'}, dimensions={1}, use_global_device_ids=true | all-gather | bytes 835584 | tf_op jit(solution)/shard_map/while/body/eval_jaxpr/all_gather | solution.py:81
  76.8 4.6 all-to-all-start.1
  93.2 3.9 collective-permute-start
  104.2 19.4 %all_gather.24 = bf16[1536,256]{0,1:T(8,128)(2,1)S(1)} all-gather(bf16[1536,16]{0,1:T(8,128)(2,1)S(1)} %bitcast_select_fusion.3), channel_id=1, replica_groups=mesh['segment'=4,'chan'=16,'dp'=8] {'chan'}, dimensions={1}, use_global_device_ids=true | all-gather | bytes 835584 | tf_op jit(solution)/shard_map/while/body/eval_jaxpr/all_gather | solution.py:81
  129.9 4.6 all-to-all-start
  142.6 18.4 %all_gather.25 = bf16[1536,256]{0,1:T(8,128)(2,1)S(1)} all-gather(bf16[1536,16]{0,1:T(8,128)(2,1)S(1)} %add_convert_fusion.4), channel_id=1, replica_groups=mesh['segment'=4,'chan'=16,'dp'=8] {'chan'}, dimensions={1}, use_global_device_ids=true | all-gather | bytes 835584 | tf_op jit(solution)/shard_map/while/body/eval_jaxpr/all_gather | solution.py:81
  166.3 4.6 all-to-all-start.1
  182.6 3.9 collective-permute-start
  193.7 19.4 %all_gather.24 = bf16[1536,256]{0,1:T(8,128)(2,1)S(1)} all-gather(bf16[1536,16]{0,1:T(8,128)(2,1)S(1)} %bitcast_select_fusion.3), channel_id=1, replica_groups=mesh['segment'=4,'chan'=16,'dp'=8] {'chan'}, dimensions={1}, use_global_device_ids=true | all-gather | bytes 835584 | tf_op jit(solution)/shard_map/while/body/eval_jaxpr/all_gather | solution.py:81
  219.4 4.6 all-to-all-start
  232.1 18.4 %all_gather.25 = bf16[1536,256]{0,1:T(8,128)(2,1)S(1)} all-gather(bf16[1536,16]{0,1:T(8,128)(2,1)S(1)} %add_convert_fusion.4), channel_id=1, replica_groups=mesh['segment'=4,'chan'=16,'dp'=8] {'chan'}, dimensions={1}, use_global_device_ids=true | all-gather | bytes 835584 | tf_op jit(solution)/shard_map/while/body/eval_jaxpr/all_gather | solution.py:81
  255.7 4.6 all-to-all-start.1
  272.1 3.9 collective-permute-start
  283.1 19.4 %all_gather.24 = bf16[1536,256]{0,1:T(8,128)(2,1)S(1)} all-gather(bf16[1536,16]{0,1:T(8,128)(2,1)S(1)} %bitcast_select_fusion.3), channel_id=1, replica_groups=mesh['segment'=4,'chan'=16,'dp'=8] {'chan'}, dimensions={1}, use_global_device_ids=true | all-gather | bytes 835584 | tf_op jit(solution)/shard_map/while/body/eval_jaxpr/all_gather | solution.py:81
  308.8 4.6 all-to-all-start
  321.5 18.4 %all_gather.25 = bf16[1536,256]{0,1:T(8,128)(2,1)S(1)} all-gather(bf16[1536,16]{0,1:T(8,128)(2,1)S(1)} %add_convert_fusion.4), channel_id=1, replica_groups=mesh['segment'=4,'chan'=16,'dp'=8] {'chan'}, dimensions={1}, use_global_device_ids=true | all-gather | bytes 835584 | tf_op jit(solution)/shard_map/while/body/eval_jaxpr/all_gather | solution.py:81
  345.1 4.6 all-to-all-start.1
  361.5 3.9 collective-permute-start
  369.9 23.8 %all-reduce.18 = (f32[1,2,96]{2,1,0:T(2,128)}, f32[1,2,96]{2,1,0:T(2,128)}) all-reduce(f32[1,2,96]{2,1,0:T(2,128)S(1)} %bitcast.586, f32[1,2,96]{2,1,0:T(2,128)S(1)} %bitcast.587), channel_id=1, replica_groups=mesh['segment'=4,'chan'=16,'dp'=8] {'dp'}, use_global_device_ids=true, to_apply=%region_24.25 | all-reduce | flops 384 | bytes 3072 | tf_op jit(solution)/shard_map/psum | solution.py:160
  393.7 65.7 %all-reduce.22.cloned.1.call-done = (f32[1,2,96,1536]{3,2,1,0:T(8,128)}, f32[1,2,96,432]{3,2,1,0:T(8,128)}) async-done(((f32[1,2,96,1536]{3,2,1,0:T(8,128)}, f32[1,2,96,432]{3,2,1,0:T(8,128)}), (f32[1,2,96,1536]{3,2,1,0:T(8,128)}, f32[1,2,96,432]{3,2,1,0:T(8,128)})) %all-reduce.22.cloned.1.call-update) | async-done | bytes 1511440 | tf_op jit(solution)/shard_map/psum | solution.py:160
  459.4 2.4 copy.207
  (707 shorter events, 156.7 us)
Async XLA Ops:
  7.2 452.2 %all-reduce.22.cloned.1.call-start = ((), (), s32[]{:S(2)}) async-start(), calls=%async_computation.2 | async-start | bytes 3145728 | tf_op jit(solution)/shard_map/psum | solution.py:160
  9.7 29.8 %copy-start.30 = (pred[256]{0:T(512)(128)(4,1)}, pred[256]{0:T(512)(128)(4,1)S(1)}, u32[]{:S(2)}) copy-start(pred[256]{0:T(512)(128)(4,1)S(1)} %compare_and_fusion.7) | copy-start | bytes 772 | tf_op jit(solution)/shard_map/while
  9.7 29.8 %copy-start.27 = (pred[256]{0:T(512)(128)(4,1)}, pred[256]{0:T(512)(128)(4,1)S(1)}, u32[]{:S(2)}) copy-start(pred[256]{0:T(512)(128)(4,1)S(1)} %compare_and_fusion.8) | copy-start | bytes 772 | tf_op jit(solution)/shard_map/while
  40.7 12.3 %all-to-all-start = ((bf16[96,16,16]{0,2,1:T(8,128)(2,1)}), bf16[96,16,16]{0,2,1:T(8,128)(2,1)S(1)}, u32[]{:S(2)}, u32[]{:S(2)}) async-start(bf16[96,16,16]{0,2,1:T(8,128)(2,1)} %convert_element_type.430), calls=%async_computation | async-start | bytes 131072 | tf_op jit(solution)/shard_map/while/body/eval_jaxpr/all_to_all | solution.py:87
  76.8 14.7 %all-to-all-start.1 = ((bf16[96,16,16]{0,2,1:T(8,128)(2,1)}), bf16[96,16,16]{0,2,1:T(8,128)(2,1)S(1)}, u32[]{:S(2)}, u32[]{:S(2)}) async-start(bf16[96,16,16]{0,2,1:T(8,128)(2,1)} %convert_element_type.431), calls=%async_computation.1 | async-start | bytes 131072 | tf_op jit(solution)/shard_map/while/body/eval_jaxpr/all_to_all | solution.py:87
  93.2 6.0 %collective-permute-start = (bf16[1536,16]{0,1:T(8,128)(2,1)S(1)}, bf16[1536,16]{0,1:T(8,128)(2,1)S(1)}, u32[]{:S(2)}, u32[]{:S(2)}) collective-permute-start(bf16[1536,16]{0,1:T(8,128)(2,1)S(1)} %get-tuple-element.790), channel_id=1, source_target_pairs={{128,0},{256,128},{384,256},{129,1},{257,129},{385,257},{130,2},{2... | collective-permute-start | bytes 147464 | tf_op jit(solution)/shard_map/while/body/eval_jaxpr/ppermute | solution.py:14
  99.2 29.5 %copy-start.30 = (pred[256]{0:T(512)(128)(4,1)}, pred[256]{0:T(512)(128)(4,1)S(1)}, u32[]{:S(2)}) copy-start(pred[256]{0:T(512)(128)(4,1)S(1)} %compare_and_fusion.7) | copy-start | bytes 772 | tf_op jit(solution)/shard_map/while
  99.2 29.5 %copy-start.27 = (pred[256]{0:T(512)(128)(4,1)}, pred[256]{0:T(512)(128)(4,1)S(1)}, u32[]{:S(2)}) copy-start(pred[256]{0:T(512)(128)(4,1)S(1)} %compare_and_fusion.8) | copy-start | bytes 772 | tf_op jit(solution)/shard_map/while
  129.9 12.5 %all-to-all-start = ((bf16[96,16,16]{0,2,1:T(8,128)(2,1)}), bf16[96,16,16]{0,2,1:T(8,128)(2,1)S(1)}, u32[]{:S(2)}, u32[]{:S(2)}) async-start(bf16[96,16,16]{0,2,1:T(8,128)(2,1)} %convert_element_type.430), calls=%async_computation | async-start | bytes 131072 | tf_op jit(solution)/shard_map/while/body/eval_jaxpr/all_to_all | solution.py:87
  141.4 19.6 %copy-start.22 = (f32[96]{0:T(128)S(1)}, f32[96]{0:T(128)}, u32[]{:S(2)}) copy-start(f32[96]{0:T(128)} %mul.953) | copy-start | bytes 1156 | tf_op jit(solution)/shard_map/while
  166.3 14.7 %all-to-all-start.1 = ((bf16[96,16,16]{0,2,1:T(8,128)(2,1)}), bf16[96,16,16]{0,2,1:T(8,128)(2,1)S(1)}, u32[]{:S(2)}, u32[]{:S(2)}) async-start(bf16[96,16,16]{0,2,1:T(8,128)(2,1)} %convert_element_type.431), calls=%async_computation.1 | async-start | bytes 131072 | tf_op jit(solution)/shard_map/while/body/eval_jaxpr/all_to_all | solution.py:87
  182.6 6.0 %collective-permute-start = (bf16[1536,16]{0,1:T(8,128)(2,1)S(1)}, bf16[1536,16]{0,1:T(8,128)(2,1)S(1)}, u32[]{:S(2)}, u32[]{:S(2)}) collective-permute-start(bf16[1536,16]{0,1:T(8,128)(2,1)S(1)} %get-tuple-element.790), channel_id=1, source_target_pairs={{128,0},{256,128},{384,256},{129,1},{257,129},{385,257},{130,2},{2... | collective-permute-start | bytes 147464 | tf_op jit(solution)/shard_map/while/body/eval_jaxpr/ppermute | solution.py:14
  188.6 29.5 %copy-start.30 = (pred[256]{0:T(512)(128)(4,1)}, pred[256]{0:T(512)(128)(4,1)S(1)}, u32[]{:S(2)}) copy-start(pred[256]{0:T(512)(128)(4,1)S(1)} %compare_and_fusion.7) | copy-start | bytes 772 | tf_op jit(solution)/shard_map/while
  188.7 29.5 %copy-start.27 = (pred[256]{0:T(512)(128)(4,1)}, pred[256]{0:T(512)(128)(4,1)S(1)}, u32[]{:S(2)}) copy-start(pred[256]{0:T(512)(128)(4,1)S(1)} %compare_and_fusion.8) | copy-start | bytes 772 | tf_op jit(solution)/shard_map/while
  219.4 12.5 %all-to-all-start = ((bf16[96,16,16]{0,2,1:T(8,128)(2,1)}), bf16[96,16,16]{0,2,1:T(8,128)(2,1)S(1)}, u32[]{:S(2)}, u32[]{:S(2)}) async-start(bf16[96,16,16]{0,2,1:T(8,128)(2,1)} %convert_element_type.430), calls=%async_computation | async-start | bytes 131072 | tf_op jit(solution)/shard_map/while/body/eval_jaxpr/all_to_all | solution.py:87
  230.9 19.6 %copy-start.22 = (f32[96]{0:T(128)S(1)}, f32[96]{0:T(128)}, u32[]{:S(2)}) copy-start(f32[96]{0:T(128)} %mul.953) | copy-start | bytes 1156 | tf_op jit(solution)/shard_map/while
  255.7 14.7 %all-to-all-start.1 = ((bf16[96,16,16]{0,2,1:T(8,128)(2,1)}), bf16[96,16,16]{0,2,1:T(8,128)(2,1)S(1)}, u32[]{:S(2)}, u32[]{:S(2)}) async-start(bf16[96,16,16]{0,2,1:T(8,128)(2,1)} %convert_element_type.431), calls=%async_computation.1 | async-start | bytes 131072 | tf_op jit(solution)/shard_map/while/body/eval_jaxpr/all_to_all | solution.py:87
  272.1 6.0 %collective-permute-start = (bf16[1536,16]{0,1:T(8,128)(2,1)S(1)}, bf16[1536,16]{0,1:T(8,128)(2,1)S(1)}, u32[]{:S(2)}, u32[]{:S(2)}) collective-permute-start(bf16[1536,16]{0,1:T(8,128)(2,1)S(1)} %get-tuple-element.790), channel_id=1, source_target_pairs={{128,0},{256,128},{384,256},{129,1},{257,129},{385,257},{130,2},{2... | collective-permute-start | bytes 147464 | tf_op jit(solution)/shard_map/while/body/eval_jaxpr/ppermute | solution.py:14
  278.1 29.5 %copy-start.30 = (pred[256]{0:T(512)(128)(4,1)}, pred[256]{0:T(512)(128)(4,1)S(1)}, u32[]{:S(2)}) copy-start(pred[256]{0:T(512)(128)(4,1)S(1)} %compare_and_fusion.7) | copy-start | bytes 772 | tf_op jit(solution)/shard_map/while
  278.1 29.5 %copy-start.27 = (pred[256]{0:T(512)(128)(4,1)}, pred[256]{0:T(512)(128)(4,1)S(1)}, u32[]{:S(2)}) copy-start(pred[256]{0:T(512)(128)(4,1)S(1)} %compare_and_fusion.8) | copy-start | bytes 772 | tf_op jit(solution)/shard_map/while
  308.8 12.5 %all-to-all-start = ((bf16[96,16,16]{0,2,1:T(8,128)(2,1)}), bf16[96,16,16]{0,2,1:T(8,128)(2,1)S(1)}, u32[]{:S(2)}, u32[]{:S(2)}) async-start(bf16[96,16,16]{0,2,1:T(8,128)(2,1)} %convert_element_type.430), calls=%async_computation | async-start | bytes 131072 | tf_op jit(solution)/shard_map/while/body/eval_jaxpr/all_to_all | solution.py:87
  320.3 19.6 %copy-start.22 = (f32[96]{0:T(128)S(1)}, f32[96]{0:T(128)}, u32[]{:S(2)}) copy-start(f32[96]{0:T(128)} %mul.953) | copy-start | bytes 1156 | tf_op jit(solution)/shard_map/while
  345.1 14.7 %all-to-all-start.1 = ((bf16[96,16,16]{0,2,1:T(8,128)(2,1)}), bf16[96,16,16]{0,2,1:T(8,128)(2,1)S(1)}, u32[]{:S(2)}, u32[]{:S(2)}) async-start(bf16[96,16,16]{0,2,1:T(8,128)(2,1)} %convert_element_type.431), calls=%async_computation.1 | async-start | bytes 131072 | tf_op jit(solution)/shard_map/while/body/eval_jaxpr/all_to_all | solution.py:87
  361.5 6.0 %collective-permute-start = (bf16[1536,16]{0,1:T(8,128)(2,1)S(1)}, bf16[1536,16]{0,1:T(8,128)(2,1)S(1)}, u32[]{:S(2)}, u32[]{:S(2)}) collective-permute-start(bf16[1536,16]{0,1:T(8,128)(2,1)S(1)} %get-tuple-element.790), channel_id=1, source_target_pairs={{128,0},{256,128},{384,256},{129,1},{257,129},{385,257},{130,2},{2... | collective-permute-start | bytes 147464 | tf_op jit(solution)/shard_map/while/body/eval_jaxpr/ppermute | solution.py:14
  (109 other events, 477.3 us)
Sparse Core Ops, SparseCore 0:
  370.0 89.2 all-reduce.21
where the time goes:
time: 472 us; the launch traced here: 469 us
  blocking collectives  175 us (37%)
  waiting for transfers between devices  77.5 us (16%)
  matrix products  66.1 us (14%)
  local copies, waits for them, and re-layouts  56 us (12%)
  starting transfers between devices  52.6 us (11%)
  other arithmetic  25.2 us (5%)
  between operations  14.1 us (3%)
    all_gather x8, blocking collectives, block_sharded(): grad_piece = lax.all_gather(grad_slab, 'chan', axis=1, tiled=True)  152 us
    psum x1, waiting for transfers between devices, per_device(): lax.psum((final[2], final[3], final[4], final[5]), 'dp')  65.7 us
    dot_general x72, matrix products, conv_backward(): jnp.einsum('gop,gjp->goj', grad_pre, source, preferred_element_type=jnp.f...  36.9 us
    all_to_all x8, starting transfers between devices, block_sharded(): lax.all_to_all(branch, 'chan', split_axis=1, concat_axis=0, tiled=True)  36.9 us
    psum x1, blocking collectives, per_device(): lax.psum((final[2], final[3], final[4], final[5]), 'dp')  23.8 us
    dot_general x8, matrix products, block_sharded(): fresh = jnp.dot(w_proj, grad_piece, preferred_element_type=jnp.float32)  16 us
    ppermute x4, starting transfers between devices, passed_along(): return lax.ppermute(block, axis, route)  15.7 us
    dot_general x72, matrix products, conv_backward(): jnp.einsum('goj,gop->gjp', taps_w[:, :, tap_at, :], grad_pre, preferred_e...  10.6 us
  transfers between devices with their start and end apart: 13, of which 9 were waited for; matrix products, arithmetic and copies ran while one was open for 13% of the time, Pallas kernels for 0%

commit v1 on v0

--- a/solution.py
+++ b/solution.py
@@ -78,7 +78,20 @@
 def block_sharded(grad_slab, saved_in, saved_pre, w_proj, w_conv, gain_vec, bias_vec):
     norm_state = norm_forward(saved_pre, gain_vec, bias_vec)
     act_bf = norm_state[5]
-    grad_piece = lax.all_gather(grad_slab, "chan", axis=1, tiled=True)
+    many = jax.lax.psum(1, axis_name="chan")
+    rack = [(i0, (i0 + 1) % many) for i0 in range(many)]
+    queue = [(i0, (i0 - 1) % many) for i0 in range(many)]
+    view_out, even = ([grad_slab], [grad_slab])
+    for _ in range(many // 2):
+        after = jax.lax.ppermute(view_out[-1], axis_name="chan", perm=rack)
+        view_out.append(after)
+    for _ in [*range((many - 1) // 2)]:
+        val2 = jax.lax.ppermute(even[-1], axis_name="chan", perm=queue)
+        even.append(val2)
+    state_now = jnp.concatenate([*view_out[::-1], *even[1:]], axis=1)
+    grad_piece = jnp.roll(
+        state_now, (jax.lax.axis_index("chan") - many // 2) * grad_slab.shape[1], axis=1
+    )
     fresh = jnp.dot(w_proj, grad_piece, preferred_element_type=jnp.float32)
     weight_acc = lax.dot_general(
         act_bf, grad_piece, (((1,), (1,)), ((), ())), preferred_element_type=jnp.float32

time: 472 us -> 636 us (1.35)
  starting transfers between devices: 52.6 us -> 222 us
  blocking collectives: 175 us -> 23.3 us
  waiting for transfers between devices: 77.5 us -> 222 us
  matrix products: 66.1 us -> 47.3 us
  local copies, waits for them, and re-layouts: 56 us -> 68.1 us
    ppermute x0 -> x120, starting transfers between devices: none -> 168 us  [the longest x56 166 us: block_sharded(): val2 = jax.lax.ppermute(even[-1], axis_name='chan', perm=queue)]
    all_gather x8 -> x0, blocking collectives: 152 us -> none  [block_sharded(): grad_piece = lax.all_gather(grad_slab, 'chan', axis=1, tiled=True)]
    ppermute x0 -> x120, waiting for transfers between devices: none -> 108 us  [the longest x64 96.9 us: block_sharded(): after = jax.lax.ppermute(view_out[-1], axis_name='chan', perm=rack)]
    all_to_all x8, waiting for transfers between devices: 4.02 us -> 45 us  [block_sharded(): lax.all_to_all(branch, 'chan', split_axis=1, concat_axis=0, tiled=True)]
    dot_general x72, matrix products: 36.9 us -> 14.3 us  [conv_backward(): jnp.einsum('gop,gjp->goj', grad_pre, source, preferred_element_type=jnp.f...]
    while x232 -> x552, local copies, waits for them, and re-layouts: 4.38 us -> 25.4 us
    dot_general x8, matrix products: 2.62 us -> 12.4 us  [block_sharded(): lax.dot_general(act_bf, grad_piece, (((1,), (1,)), ((), ())), preferred_e...]
  transfers between devices with their start and end apart: 13 -> 133, of which waited for: 9 -> 81; matrix products, arithmetic and copies ran while one was open for 13% -> 14% of each run, Pallas kernels for 0% -> 0%
where the time goes in v1:
time: 636 us; the launch traced here: 632 us
  starting transfers between devices  222 us (35%)
  waiting for transfers between devices  222 us (35%)
  local copies, waits for them, and re-layouts  68.1 us (11%)
  matrix products  47.3 us (7%)
  other arithmetic  30.4 us (5%)
  blocking collectives  23.3 us (4%)
  between operations  14.1 us (2%)
    ppermute x56, starting transfers between devices, block_sharded(): val2 = jax.lax.ppermute(even[-1], axis_name='chan', perm=queue)  166 us
    ppermute x64, waiting for transfers between devices, block_sharded(): after = jax.lax.ppermute(view_out[-1], axis_name='chan', perm=rack)  96.9 us
    psum x1, waiting for transfers between devices, per_device(): lax.psum((final[2], final[3], final[4], final[5]), 'dp')  61.8 us
    all_to_all x8, waiting for transfers between devices, block_sharded(): lax.all_to_all(branch, 'chan', split_axis=1, concat_axis=0, tiled=True)  45 us
    all_to_all x8, starting transfers between devices, block_sharded(): lax.all_to_all(branch, 'chan', split_axis=1, concat_axis=0, tiled=True)  37.1 us
    while x552, local copies, waits for them, and re-layouts  25.4 us
    psum x1, blocking collectives, per_device(): lax.psum((final[2], final[3], final[4], final[5]), 'dp')  23.3 us
    ppermute x4, starting transfers between devices, passed_along(): return lax.ppermute(block, axis, route)  17.5 us
  transfers between devices with their start and end apart: 133, of which 81 were waited for; matrix products, arithmetic and copies ran while one was open for 14% of the time, Pallas kernels for 0%

profile of v1, /device:TPU:2, one launch (start us, length us, event | category | flops | bytes accessed | tf_op | source)
XLA Modules:
  0.0 631.7 jit_solution(10341750229059243562)
XLA Ops:
  9.6 525.8 %while.26 = (s32[]{:T(128)}, bf16[1536,16]{0,1:T(8,128)(2,1)S(1)}, bf16[1,1,1536,16]{2,3,1,0:T(8,128)(2,1)}, f32[2,96,1536]{2,1,0:T(8,128)S(1)}, f32[2,96,432]{1...) while((s32[]{:T(128)}, bf16[1536,16]{0,1:T(8,128)(2,1)S(1)}, ...), condition=%wide.region_21.23_spmd.clone, body=%wide.region_0.22_spmd.clone.sunk | while | flops 399012256 | bytes 44390616 | solution.py:171
  20.2 4.3 collective-permute-done.1
  58.7 7.5 %all-to-all-start = ((bf16[96,16,16]{0,2,1:T(8,128)(2,1)}), bf16[96,16,16]{0,2,1:T(8,128)(2,1)S(1)}, u32[]{:S(2)}, u32[]{:S(2)}) async-start(bf16[96,16,16]{0,2,1:T(8,128)(2,1)} %convert_element_type.430), calls=%async_computation | async-start | bytes 131072 | tf_op jit(solution)/shard_map/while/body/eval_jaxpr/all_to_all | solution.py:100
  66.7 7.4 %all-to-all-done = bf16[96,16,16]{0,2,1:T(8,128)(2,1)S(1)} async-done(((bf16[96,16,16]{0,2,1:T(8,128)(2,1)}), bf16[96,16,16]{0,2,1:T(8,128)(2,1)S(1)}, u32[]{:S(2)}, u32[]{:S(2)}) %all-to-all-start) | async-done | bytes 49184 | tf_op jit(solution)/shard_map/while/body/eval_jaxpr/all_to_all | solution.py:100
  74.9 4.2 collective-permute-done.15
  137.3 4.7 collective-permute-start.30
  154.3 4.3 collective-permute-done.1
  192.9 4.4 all-to-all-start
  197.7 7.4 %all-to-all-done = bf16[96,16,16]{0,2,1:T(8,128)(2,1)S(1)} async-done(((bf16[96,16,16]{0,2,1:T(8,128)(2,1)}), bf16[96,16,16]{0,2,1:T(8,128)(2,1)S(1)}, u32[]{:S(2)}, u32[]{:S(2)}) %all-to-all-start) | async-done | bytes 49184 | tf_op jit(solution)/shard_map/while/body/eval_jaxpr/all_to_all | solution.py:100
  205.9 4.2 collective-permute-done.15
  255.3 4.1 all-to-all-start.1
  268.3 4.3 collective-permute-start.30
  284.9 4.3 collective-permute-done.1
  323.4 4.4 all-to-all-start
  328.3 7.4 %all-to-all-done = bf16[96,16,16]{0,2,1:T(8,128)(2,1)S(1)} async-done(((bf16[96,16,16]{0,2,1:T(8,128)(2,1)}), bf16[96,16,16]{0,2,1:T(8,128)(2,1)S(1)}, u32[]{:S(2)}, u32[]{:S(2)}) %all-to-all-start) | async-done | bytes 49184 | tf_op jit(solution)/shard_map/while/body/eval_jaxpr/all_to_all | solution.py:100
  336.4 4.2 collective-permute-done.15
  398.9 4.3 collective-permute-start.30
  415.5 4.3 collective-permute-done.1
  454.0 4.4 all-to-all-start
  458.8 7.4 %all-to-all-done = bf16[96,16,16]{0,2,1:T(8,128)(2,1)S(1)} async-done(((bf16[96,16,16]{0,2,1:T(8,128)(2,1)}), bf16[96,16,16]{0,2,1:T(8,128)(2,1)S(1)}, u32[]{:S(2)}, u32[]{:S(2)}) %all-to-all-start) | async-done | bytes 49184 | tf_op jit(solution)/shard_map/while/body/eval_jaxpr/all_to_all | solution.py:100
  467.0 4.2 collective-permute-done.15
  529.4 4.3 collective-permute-start.30
  536.6 23.3 %all-reduce.18 = (f32[1,2,96]{2,1,0:T(2,128)}, f32[1,2,96]{2,1,0:T(2,128)}) all-reduce(f32[1,2,96]{2,1,0:T(2,128)S(1)} %bitcast.574, f32[1,2,96]{2,1,0:T(2,128)S(1)} %bitcast.575), channel_id=1, replica_groups=mesh['segment'=4,'chan'=16,'dp'=8] {'dp'}, use_global_device_ids=true, to_apply=%region_24.26 | all-reduce | flops 384 | bytes 3072 | tf_op jit(solution)/shard_map/psum | solution.py:173
  559.9 61.8 %all-reduce.22.cloned.1.call-done = (f32[1,2,96,1536]{3,2,1,0:T(8,128)}, f32[1,2,96,432]{3,2,1,0:T(8,128)}) async-done(((f32[1,2,96,1536]{3,2,1,0:T(8,128)}, f32[1,2,96,432]{3,2,1,0:T(8,128)}), (f32[1,2,96,1536]{3,2,1,0:T(8,128)}, f32[1,2,96,432]{3,2,1,0:T(8,128)})) %all-reduce.22.cloned.1.call-update) | async-done | bytes 1511440 | tf_op jit(solution)/shard_map/psum | solution.py:173
  (1263 shorter events, 422.1 us)
Async XLA Ops:
  7.2 614.5 %all-reduce.22.cloned.1.call-start = ((), (), s32[]{:S(2)}) async-start(), calls=%async_computation.2 | async-start | bytes 3145728 | tf_op jit(solution)/shard_map/psum | solution.py:173
  10.5 9.3 %collective-permute-start = (bf16[1536,16]{0,1:T(8,128)(2,1)S(1)}, bf16[1536,16]{0,1:T(8,128)(2,1)S(1)}, u32[]{:S(2)}, u32[]{:S(2)}) collective-permute-start(bf16[1536,16]{0,1:T(8,128)(2,1)S(1)} %bitcast_select_fusion.3), channel_id=1, source_target_pairs={{0,8},{8,16},{16,24},{24,32},{32,40},{40,48},{48,56},{56,64},{64,7... | collective-permute-start | bytes 147464 | tf_op jit(solution)/shard_map/while/body/eval_jaxpr/ppermute | solution.py:86
  10.5 14.1 %collective-permute-start.8 = (bf16[1536,16]{0,1:T(8,128)(2,1)S(1)}, bf16[1536,16]{0,1:T(8,128)(2,1)S(1)}, u32[]{:S(2)}, u32[]{:S(2)}) collective-permute-start(bf16[1536,16]{0,1:T(8,128)(2,1)S(1)} %bitcast_select_fusion.3), channel_id=1, source_target_pairs={{0,120},{8,0},{16,8},{24,16},{32,24},{40,32},{48,40},{56,48},{64,5... | collective-permute-start | bytes 147464 | tf_op jit(solution)/shard_map/while/body/eval_jaxpr/ppermute | solution.py:89
  58.7 15.4 %all-to-all-start = ((bf16[96,16,16]{0,2,1:T(8,128)(2,1)}), bf16[96,16,16]{0,2,1:T(8,128)(2,1)S(1)}, u32[]{:S(2)}, u32[]{:S(2)}) async-start(bf16[96,16,16]{0,2,1:T(8,128)(2,1)} %convert_element_type.430), calls=%async_computation | async-start | bytes 131072 | tf_op jit(solution)/shard_map/while/body/eval_jaxpr/all_to_all | solution.py:100
  102.9 7.0 %collective-permute-start.28 = (bf16[1536,16]{0,1:T(8,128)(2,1)}, bf16[1536,16]{0,1:T(8,128)(2,1)}, u32[]{:S(2)}, u32[]{:S(2)}) collective-permute-start(bf16[1536,16]{0,1:T(8,128)(2,1)} %collective-permute-done.27), channel_id=1, source_target_pairs={{0,120},{8,0},{16,8},{24,16},{32,24},{40,32},{48,40},{56,48},{64,5... | collective-permute-start | bytes 147464 | tf_op jit(solution)/shard_map/while/body/eval_jaxpr/ppermute | solution.py:89
  110.0 8.7 %collective-permute-start.29 = (bf16[1536,16]{0,1:T(8,128)(2,1)}, bf16[1536,16]{0,1:T(8,128)(2,1)S(1)}, u32[]{:S(2)}, u32[]{:S(2)}) collective-permute-start(bf16[1536,16]{0,1:T(8,128)(2,1)} %collective-permute-done.28), channel_id=1, source_target_pairs={{0,120},{8,0},{16,8},{24,16},{32,24},{40,32},{48,40},{56,48},{64,5... | collective-permute-start | bytes 147464 | tf_op jit(solution)/shard_map/while/body/eval_jaxpr/ppermute | solution.py:89
  124.3 12.0 %all-to-all-start.1 = ((bf16[96,16,16]{0,2,1:T(8,128)(2,1)}), bf16[96,16,16]{0,2,1:T(8,128)(2,1)}, u32[]{:S(2)}, u32[]{:S(2)}) async-start(bf16[96,16,16]{0,2,1:T(8,128)(2,1)} %convert_element_type.431), calls=%async_computation.1 | async-start | bytes 131072 | tf_op jit(solution)/shard_map/while/body/eval_jaxpr/all_to_all | solution.py:100
  144.6 9.3 %collective-permute-start = (bf16[1536,16]{0,1:T(8,128)(2,1)S(1)}, bf16[1536,16]{0,1:T(8,128)(2,1)S(1)}, u32[]{:S(2)}, u32[]{:S(2)}) collective-permute-start(bf16[1536,16]{0,1:T(8,128)(2,1)S(1)} %bitcast_select_fusion.3), channel_id=1, source_target_pairs={{0,8},{8,16},{16,24},{24,32},{32,40},{40,48},{48,56},{56,64},{64,7... | collective-permute-start | bytes 147464 | tf_op jit(solution)/shard_map/while/body/eval_jaxpr/ppermute | solution.py:86
  144.6 14.1 %collective-permute-start.8 = (bf16[1536,16]{0,1:T(8,128)(2,1)S(1)}, bf16[1536,16]{0,1:T(8,128)(2,1)S(1)}, u32[]{:S(2)}, u32[]{:S(2)}) collective-permute-start(bf16[1536,16]{0,1:T(8,128)(2,1)S(1)} %bitcast_select_fusion.3), channel_id=1, source_target_pairs={{0,120},{8,0},{16,8},{24,16},{32,24},{40,32},{48,40},{56,48},{64,5... | collective-permute-start | bytes 147464 | tf_op jit(solution)/shard_map/while/body/eval_jaxpr/ppermute | solution.py:89
  192.9 12.2 %all-to-all-start = ((bf16[96,16,16]{0,2,1:T(8,128)(2,1)}), bf16[96,16,16]{0,2,1:T(8,128)(2,1)S(1)}, u32[]{:S(2)}, u32[]{:S(2)}) async-start(bf16[96,16,16]{0,2,1:T(8,128)(2,1)} %convert_element_type.430), calls=%async_computation | async-start | bytes 131072 | tf_op jit(solution)/shard_map/while/body/eval_jaxpr/all_to_all | solution.py:100
  240.9 8.7 %collective-permute-start.29 = (bf16[1536,16]{0,1:T(8,128)(2,1)}, bf16[1536,16]{0,1:T(8,128)(2,1)S(1)}, u32[]{:S(2)}, u32[]{:S(2)}) collective-permute-start(bf16[1536,16]{0,1:T(8,128)(2,1)} %collective-permute-done.28), channel_id=1, source_target_pairs={{0,120},{8,0},{16,8},{24,16},{32,24},{40,32},{48,40},{56,48},{64,5... | collective-permute-start | bytes 147464 | tf_op jit(solution)/shard_map/while/body/eval_jaxpr/ppermute | solution.py:89
  255.3 12.0 %all-to-all-start.1 = ((bf16[96,16,16]{0,2,1:T(8,128)(2,1)}), bf16[96,16,16]{0,2,1:T(8,128)(2,1)}, u32[]{:S(2)}, u32[]{:S(2)}) async-start(bf16[96,16,16]{0,2,1:T(8,128)(2,1)} %convert_element_type.431), calls=%async_computation.1 | async-start | bytes 131072 | tf_op jit(solution)/shard_map/while/body/eval_jaxpr/all_to_all | solution.py:100
  275.2 9.3 %collective-permute-start = (bf16[1536,16]{0,1:T(8,128)(2,1)S(1)}, bf16[1536,16]{0,1:T(8,128)(2,1)S(1)}, u32[]{:S(2)}, u32[]{:S(2)}) collective-permute-start(bf16[1536,16]{0,1:T(8,128)(2,1)S(1)} %bitcast_select_fusion.3), channel_id=1, source_target_pairs={{0,8},{8,16},{16,24},{24,32},{32,40},{40,48},{48,56},{56,64},{64,7... | collective-permute-start | bytes 147464 | tf_op jit(solution)/shard_map/while/body/eval_jaxpr/ppermute | solution.py:86
  275.2 14.1 %collective-permute-start.8 = (bf16[1536,16]{0,1:T(8,128)(2,1)S(1)}, bf16[1536,16]{0,1:T(8,128)(2,1)S(1)}, u32[]{:S(2)}, u32[]{:S(2)}) collective-permute-start(bf16[1536,16]{0,1:T(8,128)(2,1)S(1)} %bitcast_select_fusion.3), channel_id=1, source_target_pairs={{0,120},{8,0},{16,8},{24,16},{32,24},{40,32},{48,40},{56,48},{64,5... | collective-permute-start | bytes 147464 | tf_op jit(solution)/shard_map/while/body/eval_jaxpr/ppermute | solution.py:89
  323.4 12.2 %all-to-all-start = ((bf16[96,16,16]{0,2,1:T(8,128)(2,1)}), bf16[96,16,16]{0,2,1:T(8,128)(2,1)S(1)}, u32[]{:S(2)}, u32[]{:S(2)}) async-start(bf16[96,16,16]{0,2,1:T(8,128)(2,1)} %convert_element_type.430), calls=%async_computation | async-start | bytes 131072 | tf_op jit(solution)/shard_map/while/body/eval_jaxpr/all_to_all | solution.py:100
  364.5 7.0 %collective-permute-start.28 = (bf16[1536,16]{0,1:T(8,128)(2,1)}, bf16[1536,16]{0,1:T(8,128)(2,1)}, u32[]{:S(2)}, u32[]{:S(2)}) collective-permute-start(bf16[1536,16]{0,1:T(8,128)(2,1)} %collective-permute-done.27), channel_id=1, source_target_pairs={{0,120},{8,0},{16,8},{24,16},{32,24},{40,32},{48,40},{56,48},{64,5... | collective-permute-start | bytes 147464 | tf_op jit(solution)/shard_map/while/body/eval_jaxpr/ppermute | solution.py:89
  371.5 8.7 %collective-permute-start.29 = (bf16[1536,16]{0,1:T(8,128)(2,1)}, bf16[1536,16]{0,1:T(8,128)(2,1)S(1)}, u32[]{:S(2)}, u32[]{:S(2)}) collective-permute-start(bf16[1536,16]{0,1:T(8,128)(2,1)} %collective-permute-done.28), channel_id=1, source_target_pairs={{0,120},{8,0},{16,8},{24,16},{32,24},{40,32},{48,40},{56,48},{64,5... | collective-permute-start | bytes 147464 | tf_op jit(solution)/shard_map/while/body/eval_jaxpr/ppermute | solution.py:89
  385.8 12.0 %all-to-all-start.1 = ((bf16[96,16,16]{0,2,1:T(8,128)(2,1)}), bf16[96,16,16]{0,2,1:T(8,128)(2,1)}, u32[]{:S(2)}, u32[]{:S(2)}) async-start(bf16[96,16,16]{0,2,1:T(8,128)(2,1)} %convert_element_type.431), calls=%async_computation.1 | async-start | bytes 131072 | tf_op jit(solution)/shard_map/while/body/eval_jaxpr/all_to_all | solution.py:100
  405.7 9.3 %collective-permute-start = (bf16[1536,16]{0,1:T(8,128)(2,1)S(1)}, bf16[1536,16]{0,1:T(8,128)(2,1)S(1)}, u32[]{:S(2)}, u32[]{:S(2)}) collective-permute-start(bf16[1536,16]{0,1:T(8,128)(2,1)S(1)} %bitcast_select_fusion.3), channel_id=1, source_target_pairs={{0,8},{8,16},{16,24},{24,32},{32,40},{40,48},{48,56},{56,64},{64,7... | collective-permute-start | bytes 147464 | tf_op jit(solution)/shard_map/while/body/eval_jaxpr/ppermute | solution.py:86
  405.7 14.1 %collective-permute-start.8 = (bf16[1536,16]{0,1:T(8,128)(2,1)S(1)}, bf16[1536,16]{0,1:T(8,128)(2,1)S(1)}, u32[]{:S(2)}, u32[]{:S(2)}) collective-permute-start(bf16[1536,16]{0,1:T(8,128)(2,1)S(1)} %bitcast_select_fusion.3), channel_id=1, source_target_pairs={{0,120},{8,0},{16,8},{24,16},{32,24},{40,32},{48,40},{56,48},{64,5... | collective-permute-start | bytes 147464 | tf_op jit(solution)/shard_map/while/body/eval_jaxpr/ppermute | solution.py:89
  454.0 12.2 %all-to-all-start = ((bf16[96,16,16]{0,2,1:T(8,128)(2,1)}), bf16[96,16,16]{0,2,1:T(8,128)(2,1)S(1)}, u32[]{:S(2)}, u32[]{:S(2)}) async-start(bf16[96,16,16]{0,2,1:T(8,128)(2,1)} %convert_element_type.430), calls=%async_computation | async-start | bytes 131072 | tf_op jit(solution)/shard_map/while/body/eval_jaxpr/all_to_all | solution.py:100
  495.1 7.0 %collective-permute-start.28 = (bf16[1536,16]{0,1:T(8,128)(2,1)}, bf16[1536,16]{0,1:T(8,128)(2,1)}, u32[]{:S(2)}, u32[]{:S(2)}) collective-permute-start(bf16[1536,16]{0,1:T(8,128)(2,1)} %collective-permute-done.27), channel_id=1, source_target_pairs={{0,120},{8,0},{16,8},{24,16},{32,24},{40,32},{48,40},{56,48},{64,5... | collective-permute-start | bytes 147464 | tf_op jit(solution)/shard_map/while/body/eval_jaxpr/ppermute | solution.py:89
  502.1 8.7 %collective-permute-start.29 = (bf16[1536,16]{0,1:T(8,128)(2,1)}, bf16[1536,16]{0,1:T(8,128)(2,1)S(1)}, u32[]{:S(2)}, u32[]{:S(2)}) collective-permute-start(bf16[1536,16]{0,1:T(8,128)(2,1)} %collective-permute-done.28), channel_id=1, source_target_pairs={{0,120},{8,0},{16,8},{24,16},{32,24},{40,32},{48,40},{56,48},{64,5... | collective-permute-start | bytes 147464 | tf_op jit(solution)/shard_map/while/body/eval_jaxpr/ppermute | solution.py:89
  516.4 12.0 %all-to-all-start.1 = ((bf16[96,16,16]{0,2,1:T(8,128)(2,1)}), bf16[96,16,16]{0,2,1:T(8,128)(2,1)}, u32[]{:S(2)}, u32[]{:S(2)}) async-start(bf16[96,16,16]{0,2,1:T(8,128)(2,1)} %convert_element_type.431), calls=%async_computation.1 | async-start | bytes 131072 | tf_op jit(solution)/shard_map/while/body/eval_jaxpr/all_to_all | solution.py:100
  (327 other events, 3045.3 us)
Sparse Core Ops, SparseCore 0:
  536.7 84.9 all-reduce.21
